TPU v7x, 512 devices: a whole 4x4x16 slice. The times are simulated.
512 devices in a mesh: dp: 8 (over x_hi, y), fsdp: 16 (over z), tensor: 4 (over x_lo, core).
Axes of the slice: x: 4 (x_hi: 2, x_lo: 2; x = x_hi * 2 + x_lo), y: 4, z: 16, core: 2. Of those that a mesh axis runs over, the one named last changes fastest.
Arguments:
- grad_part: bfloat16 [8, 16, 2048, 1024], P('dp', 'fsdp', None, 'tensor'), may hold values from -900 to 900
- gain_grad_part: bfloat16 [8, 16, 4, 2048], P('dp', 'fsdp', 'tensor'), may hold values from -840 to 840
- master: float32 [2048, 1024], P('fsdp', 'tensor'), may hold values from -0.005 to 0.005
- moment_one: float32 [2048, 1024], P('fsdp', 'tensor'), may hold values from -2.4 to 2.4
- moment_two: float32 [2048, 1024], P('fsdp', 'tensor'), may hold values from 0.05 to 1.5
- teacher: float32 [2048, 1024], P('fsdp', 'tensor'), may hold values from -0.005 to 0.005
- gain_master: float32 [2048], P('fsdp'), may hold values from -0.008 to 0.008
- gain_moment_one: float32 [2048], P('fsdp'), may hold values from -18 to 18
- gain_moment_two: float32 [2048], P('fsdp'), may hold values from 2 to 32
- gain_teacher: float32 [2048], P('fsdp'), may hold values from -0.008 to 0.008
Outputs:
- weights: bfloat16 [2048, 1024], P(None, 'tensor')
- gain_weights: bfloat16 [2048], replicated
- master_new: float32 [2048, 1024], P('fsdp', 'tensor')
- moment_one_new: float32 [2048, 1024], P('fsdp', 'tensor')
- moment_two_new: float32 [2048, 1024], P('fsdp', 'tensor')
- teacher_new: float32 [2048, 1024], P('fsdp', 'tensor')
- gain_master_new: float32 [2048], P('fsdp')
- gain_moment_one_new: float32 [2048], P('fsdp')
- gain_moment_two_new: float32 [2048], P('fsdp')
- gain_teacher_new: float32 [2048], P('fsdp')
All inputs are finite; a program needn't handle non-finite values.
Results may differ from a plain program's by a relative error of at most 0.001.
Values may be sent and summed in bfloat16 or wider, within the bound.
No kernel may reach another device: no remote copies, remote signals or barrier semaphores. Data moves between devices by JAX's collectives and lax.ppermute only.
A program may use at most 64 MiB of HBM per device.

v0:
```python
import math
import jax
import jax.numpy as jnp
from jax import lax
from jax.sharding import PartitionSpec as P

D = 2048
HEADS = 8
HEAD = 128
STEP = 20
beta_one = 0.9
beta_two = 0.95
learn_rate = 0.001
teacher_keep = 0.996
clip_level = 2.0
tiny_epsilon = 1e-08


def adamw(parameter, first_moment, second_moment, gradient, clip_factor, weight_decay, shadow):
    scaled = gradient * clip_factor
    first_new = beta_one * first_moment + (1.0 - beta_one) * scaled
    second_new = beta_two * second_moment + (1.0 - beta_two) * scaled * scaled
    corr_one = 1.0 - beta_one**STEP
    corr_two = 1.0 - beta_two**STEP
    direction = first_new / corr_one / (jnp.sqrt(second_new / corr_two) + tiny_epsilon)
    parameter_new = parameter - learn_rate * (direction + weight_decay * parameter)
    shadow_new = teacher_keep * shadow + (1.0 - teacher_keep) * parameter_new
    return (parameter_new, first_new, second_new, shadow_new)


def shards(
    grad_part,
    gain_grad_part,
    master,
    moment_one,
    moment_two,
    teacher,
    gain_master,
    gain_moment_one,
    gain_moment_two,
    gain_teacher,
):
    tensor_count = lax.axis_size("tensor")
    local_gain = gain_grad_part[0, 0, 0].astype(jnp.float32)
    local_gain = lax.psum(local_gain, "tensor")
    local_grad = grad_part[0, 0].astype(jnp.float32)
    owned_rows, owned_gain = (
        lax.psum_scatter(local_grad, "fsdp", scatter_dimension=0, tiled=True),
        lax.psum_scatter(local_gain, "fsdp", scatter_dimension=0, tiled=True),
    )
    owned_rows, owned_gain = lax.psum((owned_rows, owned_gain), "dp")
    own_squares = jnp.sum(owned_rows * owned_rows) + jnp.sum(owned_gain * owned_gain) / tensor_count
    total_squares = lax.psum(own_squares, ("fsdp", "tensor"))
    clip_limit = clip_level * math.sqrt(D * HEADS * HEAD + D)
    clip_factor = clip_limit / (jnp.sqrt(total_squares) + 1e-06)
    matrix_state = adamw(master, moment_one, moment_two, owned_rows, clip_factor, 0.1, teacher)
    gain_state = adamw(
        gain_master, gain_moment_one, gain_moment_two, owned_gain, clip_factor, 0.0, gain_teacher
    )
    weights, gain_weights = (
        lax.all_gather(matrix_state[0].astype(jnp.bfloat16), "fsdp", axis=0, tiled=True),
        lax.all_gather(gain_state[0].astype(jnp.bfloat16), "fsdp", axis=0, tiled=True),
    )
    return (
        weights,
        gain_weights,
        matrix_state[0],
        matrix_state[1],
        matrix_state[2],
        matrix_state[3],
        gain_state[0],
        gain_state[1],
        gain_state[2],
        gain_state[3],
    )


def solution(mesh):
    return jax.shard_map(
        shards,
        mesh=mesh,
        in_specs=(
            P("dp", "fsdp", None, "tensor"),
            P("dp", "fsdp", "tensor", None),
            P("fsdp", "tensor"),
            P("fsdp", "tensor"),
            P("fsdp", "tensor"),
            P("fsdp", "tensor"),
            P("fsdp"),
            P("fsdp"),
            P("fsdp"),
            P("fsdp"),
        ),
        out_specs=(
            P(None, "tensor"),
            P(),
            P("fsdp", "tensor"),
            P("fsdp", "tensor"),
            P("fsdp", "tensor"),
            P("fsdp", "tensor"),
            P("fsdp"),
            P("fsdp"),
            P("fsdp"),
            P("fsdp"),
        ),
        check_vma=False,
    )
```

profile of v0, /device:TPU:2, one launch (start us, length us, event | category | flops | bytes accessed | tf_op | source)
XLA Modules:
  0.0 377.3 jit_solution(621989605081140635)
XLA Ops:
  7.2 0.0 copy-start.5
  7.2 0.0 copy-start.2
  7.2 0.0 copy-start.3
  7.2 0.0 copy-start.4
  7.2 0.0 copy-start.1
  7.2 0.0 reduce-scatter.2.cloned.1.call-start
  7.3 2.9 bitcast_convert_fusion
  10.1 0.0 copy-start.6
  10.1 0.0 copy-start.7
  10.1 0.0 copy-start.8
  10.1 0.0 copy-start.9
  10.1 0.0 reduce-scatter.2.cloned.1.call-update
  10.2 0.0 all-reduce.3.cloned.1.call-start
  10.2 78.5 %reduce-scatter.2.cloned.1.call-done = f32[128,256]{1,0:T(8,128)} async-done(((f32[2048,256]{1,0:T(8,128)}), f32[128,256]{1,0:T(8,128)}) %reduce-scatter.2.cloned.1.call-update) | async-done | bytes 131088 | tf_op jit(solution)/shard_map/reduce_scatter | solution.py:48
  88.7 0.0 all-reduce.3.cloned.1.call-update
  88.7 0.0 all-gather.3.cloned.1.call-start
  88.8 0.0 copy-done.5
  88.8 1.3 dynamic-slice
  90.7 28.9 %all-reduce = f32[2048]{0:T(1024)S(1)} all-reduce(f32[2048]{0:T(1024)S(1)} %bitcast.8), channel_id=3, replica_groups=mesh['dp'=8,'fsdp'=16,'tensor'=4] {'fsdp'}, use_global_device_ids=true, to_apply=%region_4.0.clone | all-reduce | flops 2048 | bytes 16384
  119.6 0.1 dynamic-slice.1
  119.7 6.0 %psum.32 = f32[128]{0:T(128)S(1)} all-reduce(f32[128]{0:T(128)S(1)} %dynamic-slice.1), channel_id=1, replica_groups=mesh['dp'=8,'fsdp'=16,'tensor'=4] {'tensor'}, use_global_device_ids=true, to_apply=%region_3.0 | all-reduce | flops 128 | bytes 1024 | tf_op jit(solution)/shard_map/psum | solution.py:45
  125.7 22.9 %psum.30 = f32[128]{0:T(128)S(1)} all-reduce(f32[128]{0:T(128)S(1)} %psum.32), channel_id=1, replica_groups=mesh['dp'=8,'fsdp'=16,'tensor'=4] {'dp'}, use_global_device_ids=true, to_apply=%region_5.0 | all-reduce | flops 128 | bytes 1024 | tf_op jit(solution)/shard_map/psum | solution.py:51
  148.6 0.6 multiply_reduce_fusion.1
  149.8 38.0 %all-reduce.3.cloned.1.call-done = f32[128,256]{1,0:T(8,128)} async-done(((f32[128,256]{1,0:T(8,128)}), f32[128,256]{1,0:T(8,128)}) %all-reduce.3.cloned.1.call-update) | async-done | bytes 131088 | tf_op jit(solution)/shard_map/psum | solution.py:51
  187.8 1.5 multiply_reduce_fusion
  190.0 102.3 %psum.31 = f32[]{:T(128)} all-reduce(f32[]{:T(128)S(6)} %add.54), channel_id=1, replica_groups=mesh['dp'=8,'fsdp'=16,'tensor'=4] {'fsdp','tensor'}, use_global_device_ids=true, to_apply=%region_7.0 | all-reduce | flops 1 | bytes 8 | tf_op jit(solution)/shard_map/psum | solution.py:53
  293.0 0.0 copy-done.2
  293.0 0.0 copy-done.3
  293.0 0.0 copy-done.4
  293.0 0.0 copy-done.1
  293.0 1.7 multiply_add_fusion
  294.7 0.0 copy-start
  294.7 0.7 convert_element_type.22
  295.4 0.0 all-gather.3.cloned.1.call-update
  295.4 0.0 copy-done.6
  295.4 0.0 copy-done.7
  295.5 0.0 copy-done.8
  295.5 0.0 copy-done.9
  295.5 0.5 multiply_add_fusion.2
  296.0 0.0 copy-start.10
  296.0 29.8 %all-gather = bf16[16,1,128]{2,1,0:T(2,128)(2,1)S(1)} all-gather(bf16[1,1,128]{2,1,0:T(2,128)(2,1)S(1)} %convert_bitcast_fusion), channel_id=1, replica_groups=mesh['dp'=8,'fsdp'=16,'tensor'=4] {'fsdp'}, dimensions={0}, use_global_device_ids=true | all-gather | bytes 4352 | tf_op jit(solution)/shard_map/all_gather | solution.py:62
  325.8 0.6 reduce
  326.5 42.0 %all-gather.3.cloned.1.call-done = bf16[2048,256]{1,0:T(8,128)(2,1)} async-done(((bf16[128,256]{1,0:T(8,128)(2,1)}), bf16[2048,256]{1,0:T(8,128)(2,1)}) %all-gather.3.cloned.1.call-update) | async-done | bytes 1048592 | tf_op jit(solution)/shard_map/all_gather | solution.py:61
  368.5 2.3 copy.22
  370.8 0.0 copy-done
  370.8 0.0 copy-done.10
  (2 shorter events, 0.0 us)
Async XLA Ops:
  7.2 81.6 %copy-start.5 = (bf16[1,1,1,2048]{3,2,1,0:T(2,128)(2,1)S(1)}, bf16[1,1,1,2048]{3,2,1,0:T(2,128)(2,1)}, u32[]{:S(2)}) copy-start(bf16[1,1,1,2048]{3,2,1,0:T(2,128)(2,1)} %param.11) | copy-start | bytes 12292
  7.2 285.8 %copy-start.2 = (f32[128,256]{1,0:T(8,128)S(1)}, f32[128,256]{1,0:T(8,128)}, u32[]{:S(2)}) copy-start(f32[128,256]{1,0:T(8,128)} %param.12) | copy-start | bytes 393220
  7.2 285.8 %copy-start.3 = (f32[128,256]{1,0:T(8,128)S(1)}, f32[128,256]{1,0:T(8,128)}, u32[]{:S(2)}) copy-start(f32[128,256]{1,0:T(8,128)} %param.13) | copy-start | bytes 393220
  7.2 285.8 %copy-start.4 = (f32[128,256]{1,0:T(8,128)S(1)}, f32[128,256]{1,0:T(8,128)}, u32[]{:S(2)}) copy-start(f32[128,256]{1,0:T(8,128)} %param.14) | copy-start | bytes 393220
  7.2 285.8 %copy-start.1 = (f32[128,256]{1,0:T(8,128)S(1)}, f32[128,256]{1,0:T(8,128)}, u32[]{:S(2)}) copy-start(f32[128,256]{1,0:T(8,128)} %param.15) | copy-start | bytes 393220
  7.2 81.5 %reduce-scatter.2.cloned.1.call-start = ((), (), s32[]{:S(2)}) async-start(), calls=%async_computation.1 | async-start | bytes 2228224 | tf_op jit(solution)/shard_map/reduce_scatter | solution.py:48
  10.1 285.3 %copy-start.6 = (f32[128]{0:T(128)S(1)}, f32[128]{0:T(128)}, u32[]{:S(2)}) copy-start(f32[128]{0:T(128)} %param.19) | copy-start | bytes 1540
  10.1 285.3 %copy-start.7 = (f32[128]{0:T(128)S(1)}, f32[128]{0:T(128)}, u32[]{:S(2)}) copy-start(f32[128]{0:T(128)} %param.16) | copy-start | bytes 1540
  10.1 285.3 %copy-start.8 = (f32[128]{0:T(128)S(1)}, f32[128]{0:T(128)}, u32[]{:S(2)}) copy-start(f32[128]{0:T(128)} %param.17) | copy-start | bytes 1540
  10.1 285.3 %copy-start.9 = (f32[128]{0:T(128)S(1)}, f32[128]{0:T(128)}, u32[]{:S(2)}) copy-start(f32[128]{0:T(128)} %param.18) | copy-start | bytes 1540
  10.2 177.6 %all-reduce.3.cloned.1.call-start = ((), (), s32[]{:S(2)}) async-start(), calls=%async_computation.2 | async-start | bytes 262144 | tf_op jit(solution)/shard_map/psum | solution.py:51
  88.7 279.8 %all-gather.3.cloned.1.call-start = ((), (), s32[]{:S(2)}) async-start(), calls=%async_computation.3 | async-start | bytes 1114112 | tf_op jit(solution)/shard_map/all_gather | solution.py:61
  294.7 76.1 %copy-start = (f32[128,256]{1,0:T(8,128)}, f32[128,256]{1,0:T(8,128)S(1)}, u32[]{:S(2)}) copy-start(f32[128,256]{1,0:T(8,128)S(1)} %get-tuple-element.30) | copy-start | bytes 393220
  296.0 74.8 %copy-start.10 = (f32[128]{0:T(128)}, f32[128]{0:T(128)S(1)}, u32[]{:S(2)}) copy-start(f32[128]{0:T(128)S(1)} %get-tuple-element.34) | copy-start | bytes 1540
Sparse Core Ops, SparseCore 0:
  10.9 77.7 reduce-scatter.1
  91.6 96.1 all-reduce.2
  295.6 72.9 all-gather.2
where the time goes:
time: 378 us; the launch traced here: 377 us
  blocking collectives  190 us (50%)
  waiting for transfers between devices  159 us (42%)
  between operations  16.6 us (4%)
  other arithmetic  8.58 us (2%)
    psum x1, blocking collectives, shards(): total_squares = lax.psum(own_squares, ('fsdp', 'tensor'))  102 us
    reduce_scatter x1, waiting for transfers between devices, shards(): lax.psum_scatter(local_grad, 'fsdp', scatter_dimension=0, tiled=True)  78.5 us
    all_gather x1, waiting for transfers between devices, shards(): lax.all_gather(matrix_state[0].astype(jnp.bfloat16), 'fsdp', axis=0, tile...  42 us
    psum x1, waiting for transfers between devices, shards(): owned_rows, owned_gain = lax.psum((owned_rows, owned_gain), 'dp')  38 us
    all_gather x1, blocking collectives, shards(): lax.all_gather(gain_state[0].astype(jnp.bfloat16), 'fsdp', axis=0, tiled=...  29.8 us
    unnamed x1, blocking collectives  28.9 us
    psum x1, blocking collectives, shards(): owned_rows, owned_gain = lax.psum((owned_rows, owned_gain), 'dp')  22.9 us
  transfers between devices with their start and end apart: 3, of which 3 were waited for; matrix products, arithmetic and copies ran while one was open for 1% of the time, Pallas kernels for 0%

commit v1 on v0

--- a/solution.py
+++ b/solution.py
@@ -57,8 +57,14 @@
     gain_state = adamw(
         gain_master, gain_moment_one, gain_moment_two, owned_gain, clip_factor, 0.0, gain_teacher
     )
+
+    def show_the_quotas(mine, which_axis):
+        return jnp.concatenate(
+            lax.all_to_all(jnp.stack([mine] * lax.axis_size(which_axis)), which_axis, 0, 0), 0
+        )
+
     weights, gain_weights = (
-        lax.all_gather(matrix_state[0].astype(jnp.bfloat16), "fsdp", axis=0, tiled=True),
+        show_the_quotas(matrix_state[0].astype(jnp.bfloat16), "fsdp"),
         lax.all_gather(gain_state[0].astype(jnp.bfloat16), "fsdp", axis=0, tiled=True),
     )
     return (

time: 378 us -> 390 us (1.032)
  the two profiles are of different devices: /device:TPU:2 before, /device:TPU:32 now
where the time goes in v1:
time: 390 us; the launch traced here: 389 us
  blocking collectives  225 us (58%)
  waiting for transfers between devices  116 us (30%)
  starting transfers between devices  19.6 us (5%)
  between operations  16.9 us (4%)
  other arithmetic  7.93 us (2%)
    psum x1, blocking collectives, shards(): total_squares = lax.psum(own_squares, ('fsdp', 'tensor'))  98.4 us
    reduce_scatter x1, waiting for transfers between devices, shards(): lax.psum_scatter(local_grad, 'fsdp', scatter_dimension=0, tiled=True)  77.6 us
    all_gather x1, blocking collectives, shards(): lax.all_gather(gain_state[0].astype(jnp.bfloat16), 'fsdp', axis=0, tiled=...  68.2 us
    psum x1, waiting for transfers between devices, shards(): owned_rows, owned_gain = lax.psum((owned_rows, owned_gain), 'dp')  38.6 us
    unnamed x1, blocking collectives  28.4 us
    psum x1, blocking collectives, shards(): owned_rows, owned_gain = lax.psum((owned_rows, owned_gain), 'dp')  24.1 us
    all_to_all x1, starting transfers between devices, show_the_quotas(): lax.all_to_all(jnp.stack([mine] * lax.axis_size(which_axis)), which_axis,...  19.5 us
  transfers between devices with their start and end apart: 3, of which 2 were waited for; matrix products, arithmetic and copies ran while one was open for 1% of the time, Pallas kernels for 0%

profile of v1, /device:TPU:32, one launch (start us, length us, event | category | flops | bytes accessed | tf_op | source)
XLA Modules:
  0.0 389.2 jit_solution(686227310949529390)
XLA Ops:
  7.2 0.0 copy-start.5
  7.2 0.0 copy-start.2
  7.2 0.0 copy-start.3
  7.2 0.0 copy-start.4
  7.2 0.0 copy-start.1
  7.2 0.0 reduce-scatter.2.cloned.1.call-start
  7.3 2.9 bitcast_convert_fusion
  10.1 0.0 reduce-scatter.2.cloned.1.call-update
  10.2 0.0 all-reduce.3.cloned.1.call-start
  10.2 77.6 %reduce-scatter.2.cloned.1.call-done = f32[128,256]{1,0:T(8,128)} async-done(((f32[2048,256]{1,0:T(8,128)}), f32[128,256]{1,0:T(8,128)}) %reduce-scatter.2.cloned.1.call-update) | async-done | bytes 131088 | tf_op jit(solution)/shard_map/reduce_scatter | solution.py:48
  87.8 0.0 all-reduce.3.cloned.1.call-update
  87.9 0.0 copy-done.5
  87.9 1.3 dynamic-slice
  89.8 28.4 %all-reduce = f32[2048]{0:T(1024)S(1)} all-reduce(f32[2048]{0:T(1024)S(1)} %bitcast.10), channel_id=3, replica_groups=mesh['dp'=8,'fsdp'=16,'tensor'=4] {'fsdp'}, use_global_device_ids=true, to_apply=%region_4.0.clone | all-reduce | flops 2048 | bytes 16384
  118.3 0.1 dynamic-slice.1
  118.4 6.0 %psum.32 = f32[128]{0:T(128)S(1)} all-reduce(f32[128]{0:T(128)S(1)} %dynamic-slice.1), channel_id=1, replica_groups=mesh['dp'=8,'fsdp'=16,'tensor'=4] {'tensor'}, use_global_device_ids=true, to_apply=%region_3.0 | all-reduce | flops 128 | bytes 1024 | tf_op jit(solution)/shard_map/psum | solution.py:45
  124.4 24.1 %psum.30 = f32[128]{0:T(128)S(1)} all-reduce(f32[128]{0:T(128)S(1)} %psum.32), channel_id=1, replica_groups=mesh['dp'=8,'fsdp'=16,'tensor'=4] {'dp'}, use_global_device_ids=true, to_apply=%region_5.0 | all-reduce | flops 128 | bytes 1024 | tf_op jit(solution)/shard_map/psum | solution.py:51
  148.5 0.6 multiply_reduce_fusion.1
  149.8 38.6 %all-reduce.3.cloned.1.call-done = f32[128,256]{1,0:T(8,128)} async-done(((f32[128,256]{1,0:T(8,128)}), f32[128,256]{1,0:T(8,128)}) %all-reduce.3.cloned.1.call-update) | async-done | bytes 131088 | tf_op jit(solution)/shard_map/psum | solution.py:51
  188.3 1.5 multiply_reduce_fusion
  190.5 98.4 %psum.31 = f32[]{:T(128)} all-reduce(f32[]{:T(128)S(6)} %add.54), channel_id=1, replica_groups=mesh['dp'=8,'fsdp'=16,'tensor'=4] {'fsdp','tensor'}, use_global_device_ids=true, to_apply=%region_7.0 | all-reduce | flops 1 | bytes 8 | tf_op jit(solution)/shard_map/psum | solution.py:53
  289.6 0.0 copy-done.2
  289.6 0.0 copy-done.3
  289.6 0.0 copy-done.4
  289.7 0.0 copy-done.1
  289.7 0.0 copy-start.6
  289.7 0.0 copy-start.7
  289.7 0.0 copy-start.8
  289.7 0.0 copy-start.9
  289.7 1.7 multiply_add_fusion
  291.5 0.0 copy-start
  291.5 1.1 stack.2
  292.5 19.5 %all-to-all-start = ((bf16[16,128,256]{2,1,0:T(8,128)(2,1)}), bf16[16,128,256]{2,1,0:T(8,128)(2,1)S(1)}, u32[]{:S(2)}, u32[]{:S(2)}) async-start(bf16[16,128,256]{2,1,0:T(8,128)(2,1)} %stack.2), calls=%async_computation.1 | async-start | bytes 2097152 | tf_op jit(solution)/shard_map/all_to_all | solution.py:63
  312.0 0.0 copy-done.6
  312.0 0.0 copy-done.7
  312.0 0.0 copy-done.8
  312.1 0.0 copy-done.9
  312.1 0.5 multiply_add_fusion.2
  312.6 0.0 copy-start.10
  312.6 68.2 %all-gather = bf16[16,1,128]{2,1,0:T(2,128)(2,1)S(1)} all-gather(bf16[1,1,128]{2,1,0:T(2,128)(2,1)S(1)} %convert_bitcast_fusion), channel_id=1, replica_groups=mesh['dp'=8,'fsdp'=16,'tensor'=4] {'fsdp'}, dimensions={0}, use_global_device_ids=true | all-gather | bytes 4352 | tf_op jit(solution)/shard_map/all_gather | solution.py:68
  380.8 0.6 reduce
  381.4 0.0 all-to-all-done
  381.4 1.0 copy.22
  382.4 0.0 copy-done
  382.4 0.0 copy-done.10
  (3 shorter events, 0.0 us)
Async XLA Ops:
  7.2 80.7 %copy-start.5 = (bf16[1,1,1,2048]{3,2,1,0:T(2,128)(2,1)S(1)}, bf16[1,1,1,2048]{3,2,1,0:T(2,128)(2,1)}, u32[]{:S(2)}) copy-start(bf16[1,1,1,2048]{3,2,1,0:T(2,128)(2,1)} %param.11) | copy-start | bytes 12292
  7.2 282.4 %copy-start.2 = (f32[128,256]{1,0:T(8,128)S(1)}, f32[128,256]{1,0:T(8,128)}, u32[]{:S(2)}) copy-start(f32[128,256]{1,0:T(8,128)} %param.12) | copy-start | bytes 393220
  7.2 282.4 %copy-start.3 = (f32[128,256]{1,0:T(8,128)S(1)}, f32[128,256]{1,0:T(8,128)}, u32[]{:S(2)}) copy-start(f32[128,256]{1,0:T(8,128)} %param.13) | copy-start | bytes 393220
  7.2 282.4 %copy-start.4 = (f32[128,256]{1,0:T(8,128)S(1)}, f32[128,256]{1,0:T(8,128)}, u32[]{:S(2)}) copy-start(f32[128,256]{1,0:T(8,128)} %param.14) | copy-start | bytes 393220
  7.2 282.4 %copy-start.1 = (f32[128,256]{1,0:T(8,128)S(1)}, f32[128,256]{1,0:T(8,128)}, u32[]{:S(2)}) copy-start(f32[128,256]{1,0:T(8,128)} %param.15) | copy-start | bytes 393220
  7.2 80.6 %reduce-scatter.2.cloned.1.call-start = ((), (), s32[]{:S(2)}) async-start(), calls=%async_computation.2 | async-start | bytes 2228224 | tf_op jit(solution)/shard_map/reduce_scatter | solution.py:48
  10.2 178.2 %all-reduce.3.cloned.1.call-start = ((), (), s32[]{:S(2)}) async-start(), calls=%async_computation.3 | async-start | bytes 262144 | tf_op jit(solution)/shard_map/psum | solution.py:51
  289.7 22.4 %copy-start.6 = (f32[128]{0:T(128)S(1)}, f32[128]{0:T(128)}, u32[]{:S(2)}) copy-start(f32[128]{0:T(128)} %param.19) | copy-start | bytes 1540
  289.7 22.4 %copy-start.7 = (f32[128]{0:T(128)S(1)}, f32[128]{0:T(128)}, u32[]{:S(2)}) copy-start(f32[128]{0:T(128)} %param.16) | copy-start | bytes 1540
  289.7 22.3 %copy-start.8 = (f32[128]{0:T(128)S(1)}, f32[128]{0:T(128)}, u32[]{:S(2)}) copy-start(f32[128]{0:T(128)} %param.17) | copy-start | bytes 1540
  289.7 22.3 %copy-start.9 = (f32[128]{0:T(128)S(1)}, f32[128]{0:T(128)}, u32[]{:S(2)}) copy-start(f32[128]{0:T(128)} %param.18) | copy-start | bytes 1540
  291.5 90.9 %copy-start = (f32[128,256]{1,0:T(8,128)}, f32[128,256]{1,0:T(8,128)S(1)}, u32[]{:S(2)}) copy-start(f32[128,256]{1,0:T(8,128)S(1)} %get-tuple-element.30) | copy-start | bytes 393220
  292.5 88.9 %all-to-all-start = ((bf16[16,128,256]{2,1,0:T(8,128)(2,1)}), bf16[16,128,256]{2,1,0:T(8,128)(2,1)S(1)}, u32[]{:S(2)}, u32[]{:S(2)}) async-start(bf16[16,128,256]{2,1,0:T(8,128)(2,1)} %stack.2), calls=%async_computation.1 | async-start | bytes 2097152 | tf_op jit(solution)/shard_map/all_to_all | solution.py:63
  312.6 69.8 %copy-start.10 = (f32[128]{0:T(128)}, f32[128]{0:T(128)S(1)}, u32[]{:S(2)}) copy-start(f32[128]{0:T(128)S(1)} %get-tuple-element.34) | copy-start | bytes 1540
Sparse Core Ops, SparseCore 0:
  10.9 76.9 reduce-scatter.1
  90.7 97.5 all-reduce.2
